TPU v7x, 256 devices: a whole 4x4x8 slice. The times are simulated.
256 devices in a mesh: tm: 16 (over y, x), space: 16 (over z, core).
Axes of the slice: x: 4, y: 4, z: 8, core: 2. Of those that a mesh axis runs over, the one named last changes fastest.
Arguments:
- queries: bfloat16 [98304, 2048], P(('tm', 'space')), may hold values from -8 to 8, as said below
- keys: bfloat16 [98304, 2048], P(('tm', 'space')), may hold values from -8 to 8, as said below
- values: bfloat16 [98304, 2048], P(('tm', 'space')), may hold values from -8 to 8, as said below
- cotangent: bfloat16 [98304, 2048], P(('tm', 'space')), may hold values from -8 to 8, as said below
Outputs:
- attended: bfloat16 [98304, 2048], P(('tm', 'space'))
- grad_queries: bfloat16 [98304, 2048], P(('tm', 'space'))
- grad_keys: bfloat16 [98304, 2048], P(('tm', 'space'))
- grad_values: bfloat16 [98304, 2048], P(('tm', 'space'))
Inputs may be any that keep to these rules, and one draw needn't show every extreme that they name: `queries`: Real-valued activations. `keys`: Real-valued activations. `values`: Real-valued activations. `cotangent`: Real-valued cotangents.
All inputs are finite; a program needn't handle non-finite values.
Results may differ from a plain program's by a relative error of at most 0.008.
Values may be sent and summed in bfloat16 or wider, within the bound.
A program may use at most 128 MiB of HBM per device.

v0:
```python
import jax
import jax.numpy as jnp
from jax import lax
from jax.sharding import PartitionSpec as P

HEADS = 16
HEAD_DIM = 128


HIGH = lax.Precision.HIGHEST


def entering(part, axis, combine, identity, reverse):
    count = lax.axis_size(axis)
    place = lax.axis_index(axis)
    ahead = count - 1 - place if reverse else place
    gathered = jax.tree.map(lambda a: lax.all_gather(a, axis), part)
    state = jax.tree.map(lambda a, e: jnp.zeros_like(a) + jnp.asarray(e, a.dtype), part, identity)

    def one(hop, state):
        source = count - 1 - hop if reverse else hop
        return combine(
            state, jax.tree.map(lambda a: lax.dynamic_index_in_dim(a, source, 0, False), gathered)
        )

    return lax.fori_loop(0, ahead, one, state)


def add_states(earlier, later):
    return tuple((first + second for first, second in zip(earlier, later)))


def group_prefix(parts, reverse):
    identity = tuple((jnp.zeros_like(piece) for piece in parts))
    if reverse:
        return entering(parts, "tm", add_states, identity, True)
    return entering(parts, "tm", add_states, identity, False)


def combine_states(parts, reverse):
    if reverse:
        totals = lax.psum((parts[0], parts[1], parts[2]), "space")
    else:
        totals = lax.psum((parts[0], parts[1], parts[2]), "space")
    joined = add_states(group_prefix(totals, reverse), totals)
    return (joined[0].astype(jnp.bfloat16), joined[1], joined[2])


def body(queries, keys, values, cotangent):
    row_count = queries.shape[0]
    group_len = row_count * lax.axis_size("space")
    shaped = (row_count, HEADS, HEAD_DIM)
    query_tok = queries.reshape(shaped)
    key_tok = keys.reshape(shaped)
    value_tok = values.reshape(shaped)
    grad_tok = cotangent.reshape(shaped)
    zero = jnp.zeros((), jnp.bfloat16)
    feat_q = jnp.maximum(query_tok, zero)
    feat_k = jnp.maximum(key_tok, zero)
    state_kv = jnp.einsum("thf,the->hfe", feat_k, value_tok, preferred_element_type=jnp.float32)
    key_sum = jnp.sum(feat_k, axis=0, dtype=jnp.float32)
    value_sum = jnp.sum(value_tok, axis=0, dtype=jnp.float32)
    prefix_round, prefix_ks, prefix_vs = combine_states((state_kv, key_sum, value_sum), False)
    count = ((lax.axis_index("tm") + 1) * group_len).astype(jnp.float32)
    feat_q32 = feat_q.astype(jnp.float32)
    numer = (
        jnp.einsum("thf,hfe->the", feat_q, prefix_round, preferred_element_type=jnp.float32)
        + prefix_vs[None]
    )
    denom = jnp.einsum("thf,hf->th", feat_q32, prefix_ks, precision=HIGH) + count
    attended = (numer / denom[..., None]).astype(jnp.bfloat16)
    grad_f = grad_tok.astype(jnp.float32)
    dnum = grad_f / denom[..., None]
    dnum_round = dnum.astype(jnp.bfloat16)
    ratio = jnp.sum(grad_f * numer, axis=-1) / (denom * denom)
    d_feat = (
        jnp.einsum("the,hfe->thf", dnum_round, prefix_round, preferred_element_type=jnp.float32)
        - ratio[..., None] * prefix_ks[None]
    )
    grad_q = jnp.where(query_tok > 0, d_feat, 0.0).astype(jnp.bfloat16)
    back_kv = jnp.einsum("thf,the->hfe", feat_q, dnum_round, preferred_element_type=jnp.float32)
    back_ks = -jnp.einsum("th,thf->hf", ratio, feat_q32, precision=HIGH)
    back_vs = jnp.sum(dnum, axis=0)
    suffix_rounded, suffix_ks, suffix_vs = combine_states((back_kv, back_ks, back_vs), True)
    grad_v = (
        jnp.einsum("thf,hfe->the", feat_k, suffix_rounded, preferred_element_type=jnp.float32)
        + suffix_vs[None]
    ).astype(jnp.bfloat16)
    d_key = (
        jnp.einsum("the,hfe->thf", value_tok, suffix_rounded, preferred_element_type=jnp.float32)
        + suffix_ks[None]
    )
    grad_k = jnp.where(key_tok > 0, d_key, 0.0).astype(jnp.bfloat16)
    flat = (row_count, HEADS * HEAD_DIM)
    return (
        attended.reshape(flat),
        grad_q.reshape(flat),
        grad_k.reshape(flat),
        grad_v.reshape(flat),
    )


def solution(mesh):
    in_specs = (
        P(("tm", "space"), None),
        P(("tm", "space"), None),
        P(("tm", "space"), None),
        P(("tm", "space"), None),
    )
    out_specs = (
        P(("tm", "space"), None),
        P(("tm", "space"), None),
        P(("tm", "space"), None),
        P(("tm", "space"), None),
    )
    return jax.shard_map(body, mesh=mesh, in_specs=in_specs, out_specs=out_specs, check_vma=False)
```

profile of v0, /device:TPU:1, one launch (start us, length us, event | category | flops | bytes accessed | tf_op | source)
XLA Modules:
  0.0 548.0 jit_solution(14846193569971334839)
XLA Ops:
  7.2 3.6 fusion.10
  10.9 116.2 %all-reduce.5.cloned.1.call-done = f32[16,128,128]{2,1,0:T(8,128)} async-done(((f32[16,128,128]{2,1,0:T(8,128)}), f32[16,128,128]{2,1,0:T(8,128)}) %all-reduce.5.cloned.1.call-update) | async-done | bytes 1048592 | tf_op jit(solution)/shard_map/psum | solution.py:44
  127.2 2.0 copy.31
  131.0 2.0 copy.34
  134.7 46.8 %all-reduce.1 = (f32[16,128]{1,0:T(8,128)S(1)}, f32[16,128]{1,0:T(8,128)S(1)}) all-reduce(f32[16,128]{1,0:T(8,128)S(1)} %bitcast.132, f32[16,128]{1,0:T(8,128)S(1)} %bitcast.131), channel_id=1, replica_groups=mesh['tm'=16,'space'=16] {'space'}, use_global_device_ids=true, to_apply=%region_2.0 | all-reduce | flops 4096 | bytes 32768 | tf_op jit(solution)/shard_map/psum | solution.py:44
  181.6 21.5 %all-gather.2 = f32[256,128]{1,0:T(8,128)S(1)} all-gather(f32[16,128]{1,0:T(8,128)S(1)} %get-tuple-element.204), channel_id=4, replica_groups=mesh['tm'=16,'space'=16] {'tm'}, dimensions={0}, use_global_device_ids=true | all-gather | bytes 139264 | tf_op jit(solution)/shard_map/all_gather | solution.py:17
  203.1 20.7 %all-gather.1 = f32[256,128]{1,0:T(8,128)S(1)} all-gather(f32[16,128]{1,0:T(8,128)S(1)} %get-tuple-element.203), channel_id=3, replica_groups=mesh['tm'=16,'space'=16] {'tm'}, dimensions={0}, use_global_device_ids=true | all-gather | bytes 139264 | tf_op jit(solution)/shard_map/all_gather | solution.py:17
  223.8 23.5 %all-gather.9.cloned.1.call-done = f32[256,128,128]{2,1,0:T(8,128)} async-done(((f32[16,128,128]{2,1,0:T(8,128)}), f32[256,128,128]{2,1,0:T(8,128)}) %all-gather.9.cloned.1.call-update) | async-done | bytes 16777232 | tf_op jit(solution)/shard_map/all_gather | solution.py:17
  247.5 2.5 fusion.24
  250.2 4.2 fusion.4
  256.4 134.3 %all-reduce.7.cloned.1.call-done = f32[16,128,128]{2,1,0:T(8,128)} async-done(((f32[16,128,128]{2,1,0:T(8,128)}), f32[16,128,128]{2,1,0:T(8,128)}) %all-reduce.7.cloned.1.call-update) | async-done | bytes 1048592 | tf_op jit(solution)/shard_map/psum | solution.py:42
  397.0 2.4 copy.36
  399.4 2.5 fusion.5
  401.9 4.0 fusion.2
  405.9 2.7 copy.41
  408.6 3.4 fusion.3
  412.1 2.6 copy.40
  414.6 2.0 divide_reduce_fusion
  416.6 47.3 %all-reduce = (f32[16,128]{1,0:T(8,128)S(1)}, f32[16,128]{1,0:T(8,128)S(1)}) all-reduce(f32[16,128]{1,0:T(8,128)S(1)} %neg.3, f32[16,128]{1,0:T(8,128)S(1)} %bitcast.130), channel_id=1, replica_groups=mesh['tm'=16,'space'=16] {'space'}, use_global_device_ids=true, to_apply=%region_9.10 | all-reduce | flops 4096 | bytes 32768 | tf_op jit(solution)/shard_map/psum | solution.py:42
  463.9 21.5 %all-gather.4 = f32[256,128]{1,0:T(8,128)S(1)} all-gather(f32[16,128]{1,0:T(8,128)S(1)} %get-tuple-element.201), channel_id=6, replica_groups=mesh['tm'=16,'space'=16] {'tm'}, dimensions={0}, use_global_device_ids=true | all-gather | bytes 139264 | tf_op jit(solution)/shard_map/all_gather | solution.py:17
  485.4 20.7 %all-gather.5 = f32[256,128]{1,0:T(8,128)S(1)} all-gather(f32[16,128]{1,0:T(8,128)S(1)} %get-tuple-element.202), channel_id=7, replica_groups=mesh['tm'=16,'space'=16] {'tm'}, dimensions={0}, use_global_device_ids=true | all-gather | bytes 139264 | tf_op jit(solution)/shard_map/all_gather | solution.py:17
  506.1 4.5 all-gather.11.cloned.1.call-done
  510.7 23.1 %while.31 = (s32[]{:T(128)}, f32[16,128,128]{2,1,0:T(8,128)S(1)}, f32[16,128]{1,0:T(8,128)S(1)}, f32[16,128]{1,0:T(8,128)S(1)}, s32[]{:T(128)}, /*index=5*/f32[1...) while((s32[]{:T(128)}, f32[16,128,128]{2,1,0:T(8,128)S(1)}, ...), condition=%wide.region_13.14_spmd, body=%wide.region_12.13_spmd.sunk | while | flops 266246 | bytes 3195051 | solution.py:26
  537.7 2.1 fusion
  (96 shorter events, 40.4 us)
Async XLA Ops:
  7.2 119.9 %all-reduce.5.cloned.1.call-start = ((), (), s32[]{:S(2)}) async-start(), calls=%async_computation | async-start | bytes 2097152 | tf_op jit(solution)/shard_map/psum | solution.py:44
  10.8 116.3 %copy-start.6 = (bf16[384,2048]{1,0:T(8,128)(2,1)S(1)}, bf16[384,2048]{1,0:T(8,128)(2,1)}, u32[]{:S(2)}) copy-start(bf16[384,2048]{1,0:T(8,128)(2,1)} %param.11) | copy-start | bytes 4718596
  10.8 236.5 %all-gather.9.cloned.1.call-start = ((), (), s32[]{:S(2)}) async-start(), calls=%async_computation.2 | async-start | bytes 17825792 | tf_op jit(solution)/shard_map/all_gather | solution.py:17
  127.1 263.5 %all-reduce.7.cloned.1.call-start = ((), (), s32[]{:S(2)}) async-start(), calls=%async_computation.1 | async-start | bytes 2097152 | tf_op jit(solution)/shard_map/psum | solution.py:42
  127.2 2.0 copy-start.4
  131.0 2.0 copy-start.11
  133.0 1.4 copy-start.1
  247.5 2.5 copy-start.8
  247.5 2.7 copy-start
  250.2 4.2 copy-start.9
  250.2 4.2 copy-start.3
  256.2 254.4 %all-gather.11.cloned.1.call-start = ((), (), s32[]{:S(2)}) async-start(), calls=%async_computation.3 | async-start | bytes 17825792 | tf_op jit(solution)/shard_map/all_gather | solution.py:17
  390.7 2.2 copy-start.5
  399.4 2.5 copy-start.10
  399.4 2.5 copy-start.13
  510.7 23.2 %copy-start.7 = (f32[16,128,128]{2,1,0:T(8,128)S(1)}, f32[16,128,128]{2,1,0:T(8,128)}, u32[]{:S(2)}) copy-start(f32[16,128,128]{2,1,0:T(8,128)} %all-reduce.7.cloned.1.call-done) | copy-start | bytes 3145732
  533.9 1.4 copy-start.2
  535.3 0.8 copy-start.14
  536.1 1.6 copy-start.12
Sparse Core Ops, SparseCore 0:
  11.0 116.0 all-reduce.4
  129.5 117.7 all-gather.8
  256.3 134.3 all-reduce.6
  392.9 117.6 all-gather.10
where the time goes:
time: 551 us; the launch traced here: 548 us
  waiting for transfers between devices  279 us (51%)
  blocking collectives  179 us (32%)
  other arithmetic  31 us (6%)
  local copies, waits for them, and re-layouts  23.6 us (4%)
  matrix products  21.3 us (4%)
  between operations  14.1 us (3%)
    psum x2, waiting for transfers between devices, combine_states(): totals = lax.psum((parts[0], parts[1], parts[2]), 'space')  250 us
    psum x2, blocking collectives, combine_states(): totals = lax.psum((parts[0], parts[1], parts[2]), 'space')  94.1 us
    all_gather x4, blocking collectives, entering(): gathered = jax.tree.map(lambda a: lax.all_gather(a, axis), part)  84.5 us
    all_gather x2, waiting for transfers between devices, entering(): gathered = jax.tree.map(lambda a: lax.all_gather(a, axis), part)  28 us
    add x34, other arithmetic, add_states(): return tuple((first + second for first, second in zip(earlier, later)))  22.6 us
    unnamed x35, local copies, waits for them, and re-layouts  11.5 us
  transfers between devices with their start and end apart: 4, of which 4 were waited for; matrix products, arithmetic and copies ran while one was open for 6% of the time, Pallas kernels for 0%

commit v1 on v0

v1 whole, which is shorter than its diff:
```python
import functools

import jax
import jax.numpy as jnp
from jax import lax
from jax.experimental import pallas as pl
from jax.experimental.pallas import tpu as pltpu
from jax.sharding import PartitionSpec as P

D = 128
STATE = D + 16
MESH = pl.DeviceIdType.MESH
F32 = jnp.float32
BF16 = jnp.bfloat16


def cols(head):
    return pl.ds(pl.multiple_of(head * D, D), D)


def sums_tile(key_row, value_row):
    row = lax.broadcasted_iota(jnp.int32, (16, D), 0)
    key_low = key_row - key_row.astype(BF16).astype(F32)
    value_low = value_row - value_row.astype(BF16).astype(F32)
    tile = jnp.where(row == 0, key_row, jnp.where(row == 1, key_low, 0.0))
    tile = jnp.where(row == 2, value_row, jnp.where(row == 3, value_low, tile))
    return tile.astype(BF16)


def split_sums(tile):
    return tile[0:1] + tile[1:2], tile[2:3] + tile[3:4]


def put_state(ref, matrix, key_row, value_row):
    ref[0:D, :] = matrix.astype(BF16)
    ref[D:STATE, :] = sums_tile(key_row, value_row)


def get_state(ref):
    return ref[...].astype(F32)


def put_packed(ref, packed):
    key_row, value_row = split_sums(packed[D:STATE])
    put_state(ref, packed[0:D], key_row, value_row)


def across(left, right):
    return lax.dot_general(left, right, (((0,), (0,)), ((), ())), preferred_element_type=F32)


def times(left, right):
    return jnp.dot(left, right, preferred_element_type=F32)


def times_t(left, right):
    return lax.dot_general(left, right, (((1,), (1,)), ((), ())), preferred_element_type=F32)


def kernel(
    sizes,
    q_hbm, k_hbm, v_hbm, g_hbm,
    att_hbm, gq_hbm, gk_hbm, gv_hbm,
    q_v, k_v, v_v, g_v, att_v, gq_v, gk_v, gv_v, dnum_v, ratio_v,
    own, pair_out, pair_in, z_out, z_in, x_out, x_in, y_out, y_in, total, fin,
    in_sem, out_sem, grad_sem,
    pair_ss, pair_rs, z_ss, z_rs, x_ss, x_rs, y_ss, y_rs, ag_ss, fw_ss, fin_rs,
):
    nx, ny, nz = sizes
    tm, space = lax.axis_index("tm"), lax.axis_index("space")
    y, x = lax.div(tm, nx), lax.rem(tm, nx)
    z, core = lax.div(space, 2), lax.rem(space, 2)
    partner = 2 * z + 1 - core
    rows = q_v.shape[0]

    def at_z(j):
        return 2 * j + core

    barrier = pltpu.get_barrier_semaphore()
    pl.semaphore_signal(barrier, inc=1, device_id={"space": partner}, device_id_type=MESH)
    for o in range(1, nz):
        pl.semaphore_signal(
            barrier, inc=1, device_id={"space": at_z(lax.rem(z + o, nz))}, device_id_type=MESH
        )
    for o in range(1, nx):
        pl.semaphore_signal(
            barrier, inc=1, device_id={"tm": y * nx + lax.rem(x + o, nx)}, device_id_type=MESH
        )
    for o in range(1, ny):
        pl.semaphore_signal(
            barrier, inc=1, device_id={"tm": lax.rem(y + o, ny) * nx + x}, device_id_type=MESH
        )

    def load(n, src, dst):
        return pltpu.make_async_copy(src, dst, in_sem.at[n])

    load(0, k_hbm, k_v).start()
    load(1, v_hbm, v_v).start()
    load(2, q_hbm, q_v).start()
    load(3, g_hbm, g_v).start()

    def order(i):
        half = lax.div(i + 1, 2)
        return jnp.where(lax.rem(i, 2) == 0, nz // 2 + half, nz // 2 - half)

    def remote(src, dst, ss, rs, where):
        return pltpu.make_async_remote_copy(
            src_ref=src, dst_ref=dst, send_sem=ss, recv_sem=rs, device_id=where, device_id_type=MESH
        )

    def pair_copy(d, j):
        return remote(
            pair_out.at[d, j], pair_in.at[d, j], pair_ss.at[d, j], pair_rs.at[d, j], {"space": partner}
        )

    def z_copy(d, j, slot):
        return remote(
            z_out.at[d, j], z_in.at[d, slot], z_ss.at[d, j], z_rs.at[d, slot], {"space": at_z(j)}
        )

    def x_copy(d, other, slot):
        return remote(
            x_out.at[d], x_in.at[d, slot], x_ss.at[d, other], x_rs.at[d, slot], {"tm": y * nx + other}
        )

    def y_copy(d, other, slot):
        return remote(
            y_out.at[d], y_in.at[d, slot], y_ss.at[d, other], y_rs.at[d, slot], {"tm": other * nx + x}
        )

    def gather_copy(d, j, head):
        return remote(
            fin.at[d, head], fin.at[d, head], ag_ss.at[d, j], fin_rs.at[d, head], {"space": at_z(j)}
        )

    def forward_copy(d, j, head):
        return remote(
            fin.at[d, head], fin.at[d, head], fw_ss.at[d, j], fin_rs.at[d, head], {"space": partner}
        )

    def give_pair(d, j, state):
        put_state(pair_out.at[d, j], *state)
        pair_copy(d, j).start()

    def keep_own(j, state):
        matrix, key_row, value_row = state
        row = lax.broadcasted_iota(jnp.int32, (16, D), 0)
        own[j, 0:D, :] = matrix
        own[j, D:STATE, :] = jnp.where(row == 0, key_row, jnp.where(row == 2, value_row, 0.0))

    def to_owner(d, off):
        j = lax.rem(z + off, nz)
        pair_copy(d, j).wait_recv()
        chip = own[j] + get_state(pair_in.at[d, j])

        @pl.when(off != 0)
        def _():
            put_packed(z_out.at[d, j], chip)
            z_copy(d, j, z).start()

        @pl.when(off == 0)
        def _():
            put_packed(z_in.at[d, z], chip)

    def scan(d):
        group = get_state(z_in.at[d, z])
        for o in range(1, nz):
            j = lax.rem(z + o, nz)
            z_copy(d, j, j).wait_recv()
            group = group + get_state(z_in.at[d, j])
        put_packed(x_out.at[d], group)
        for o in (2, 1, 3) if nx == 4 else range(1, nx):
            x_copy(d, lax.rem(x + o, nx), x).start()
        row_sum = group
        total[...] = group
        for o in range(1, nx):
            other = lax.rem(x + o, nx)
            x_copy(d, other, other).wait_recv()
            block = get_state(x_in.at[d, other])
            row_sum = row_sum + block
            before = other < x if d == 0 else other > x

            @pl.when(before)
            def _():
                total[...] += block

        put_packed(y_out.at[d], row_sum)
        for o in (2, 1, 3) if ny == 4 else range(1, ny):
            other = lax.rem(y + o, ny)

            @pl.when(other > y if d == 0 else other < y)
            def _():
                y_copy(d, other, y).start()

        for o in range(1, ny):
            other = lax.rem(y + o, ny)

            @pl.when(other < y if d == 0 else other > y)
            def _():
                y_copy(d, other, other).wait_recv()
                total[...] += get_state(y_in.at[d, other])

        put_packed(fin.at[d, space], total[...])
        forward_copy(d, z, space).start()

        def send(i, carry):
            gather_copy(d, lax.rem(z + order(i), nz), space).start()
            return carry

        lax.fori_loop(0, nz - 1, send, 0)

    def receive(d, off):
        j = lax.rem(z + off, nz)

        @pl.when(off != 0)
        def _():
            gather_copy(d, j, at_z(j)).wait_recv()
            forward_copy(d, j, at_z(j)).start()

    def receive_pair(d, off):
        j = lax.rem(z + off, nz)
        forward_copy(d, j, 2 * j + 1 - core).wait_recv()

    load(0, k_hbm, k_v).wait()
    load(1, v_hbm, v_v).wait()
    pl.semaphore_wait(barrier, 1 + (nz - 1) + (nx - 1) + (ny - 1))

    def state_of(head):
        keys, values = k_v[:, cols(head)], v_v[:, cols(head)]
        feat = jnp.maximum(keys, jnp.zeros_like(keys))
        return (
            across(feat, values),
            jnp.sum(feat.astype(F32), axis=0, keepdims=True),
            jnp.sum(values.astype(F32), axis=0, keepdims=True),
        )

    def state_step(i, carry):
        j = lax.rem(z + order(i), nz)
        give_pair(0, j, state_of(2 * j + 1 - core))
        keep_own(j, state_of(at_z(j)))

        @pl.when(i > 0)
        def _():
            to_owner(0, order(i - 1))

        return carry

    lax.fori_loop(0, nz, state_step, 0)
    to_owner(0, order(jnp.int32(nz - 1)))
    load(2, q_hbm, q_v).wait()
    load(3, g_hbm, g_v).wait()
    scan(0)

    count = ((tm + 1) * (rows * 2 * nz)).astype(F32)

    def attend(head):
        here = cols(head)
        queries, grad = q_v[:, here], g_v[:, here].astype(F32)
        feat = jnp.maximum(queries, jnp.zeros_like(queries))
        feat32 = feat.astype(F32)
        key_row, value_row = split_sums(fin[0, head, D:STATE, :].astype(F32))
        numer = times(feat, fin[0, head, 0:D, :]) + value_row
        denom = jnp.sum(feat32 * key_row, axis=1, keepdims=True) + count
        inverse = 1.0 / denom
        att_v[:, here] = (numer * inverse).astype(BF16)
        dnum = grad * inverse
        dnum_round = dnum.astype(BF16)
        dnum_v[:, here] = dnum_round
        ratio = jnp.sum(grad * numer, axis=1, keepdims=True) * (inverse * inverse)
        ratio_v[head] = ratio
        return (
            across(feat, dnum_round),
            -jnp.sum(ratio * feat32, axis=0, keepdims=True),
            jnp.sum(dnum, axis=0, keepdims=True),
        )

    def attend_step(n, carry):
        i = nz - 1 - n
        off = order(i)
        j = lax.rem(z + off, nz)
        receive(0, off)
        keep_own(j, attend(at_z(j)))
        receive_pair(0, off)
        give_pair(1, j, attend(2 * j + 1 - core))

        @pl.when(n > 0)
        def _():
            to_owner(1, order(i + 1))

        return carry

    lax.fori_loop(0, nz, attend_step, 0)
    to_owner(1, order(jnp.int32(0)))
    pltpu.make_async_copy(att_v, att_hbm, out_sem.at[0]).start()

    def query_step(head, carry):
        here = cols(head)
        key_row, _ = split_sums(fin[0, head, D:STATE, :].astype(F32))
        d_feat = times_t(dnum_v[:, here], fin[0, head, 0:D, :]) - ratio_v[head] * key_row
        gq_v[:, here] = jnp.where(q_v[:, here].astype(F32) > 0, d_feat, 0.0).astype(BF16)
        return carry

    lax.fori_loop(0, 2 * nz, query_step, 0)
    pltpu.make_async_copy(gq_v, gq_hbm, out_sem.at[1]).start()
    scan(1)

    def key_value(head):
        here = cols(head)
        keys, values = k_v[:, here], v_v[:, here]
        feat = jnp.maximum(keys, jnp.zeros_like(keys))
        matrix = fin[1, head, 0:D, :]
        key_row, value_row = split_sums(fin[1, head, D:STATE, :].astype(F32))
        gv_v[:, here] = (times(feat, matrix) + value_row).astype(BF16)
        d_key = times_t(values, matrix) + key_row
        gk_v[:, here] = jnp.where(keys.astype(F32) > 0, d_key, 0.0).astype(BF16)

    def grad_copy(j, which):
        here = pl.ds(pl.multiple_of(j * 2 * D, 2 * D), 2 * D)
        src, dst = ((gk_v, gk_hbm), (gv_v, gv_hbm))[which]
        return pltpu.make_async_copy(src.at[:, here], dst.at[:, here], grad_sem.at[which, j])

    def key_value_step(n, carry):
        off = order(nz - 1 - n)
        j = lax.rem(z + off, nz)
        receive(1, off)
        key_value(at_z(j))
        receive_pair(1, off)
        key_value(2 * j + 1 - core)
        grad_copy(j, 0).start()
        grad_copy(j, 1).start()
        return carry

    lax.fori_loop(0, nz, key_value_step, 0)

    for d in (0, 1):

        def sent(i, carry):
            off = order(i)
            j = lax.rem(z + off, nz)
            pair_copy(d, j).wait_send()
            forward_copy(d, j, at_z(j)).wait_send()

            @pl.when(off != 0)
            def _():
                z_copy(d, j, z).wait_send()
                gather_copy(d, j, space).wait_send()

            return carry

        lax.fori_loop(0, nz, sent, 0)
        for o in range(1, nx):
            x_copy(d, lax.rem(x + o, nx), x).wait_send()
        for o in range(1, ny):
            other = lax.rem(y + o, ny)

            @pl.when(other > y if d == 0 else other < y)
            def _():
                y_copy(d, other, y).wait_send()

    pltpu.make_async_copy(att_v, att_hbm, out_sem.at[0]).wait()
    pltpu.make_async_copy(gq_v, gq_hbm, out_sem.at[1]).wait()

    def stored(j, carry):
        grad_copy(j, 0).wait()
        grad_copy(j, 1).wait()
        return carry

    lax.fori_loop(0, nz, stored, 0)


def body(sizes, queries, keys, values, cotangent):
    nx, ny, nz = sizes
    heads = 2 * nz
    rows, width = queries.shape
    whole = pltpu.VMEM((rows, width), BF16)
    dma = pltpu.SemaphoreType.DMA
    like = jax.ShapeDtypeStruct((rows, width), BF16)
    return pl.pallas_call(
        functools.partial(kernel, sizes),
        out_shape=(like,) * 4,
        in_specs=[pl.BlockSpec(memory_space=pl.ANY)] * 4,
        out_specs=(pl.BlockSpec(memory_space=pl.ANY),) * 4,
        scratch_shapes=[whole] * 9
        + [
            pltpu.VMEM((heads, rows, 1), F32),
            pltpu.VMEM((nz, STATE, D), F32),
            pltpu.VMEM((2, nz, STATE, D), BF16),
            pltpu.VMEM((2, nz, STATE, D), BF16),
            pltpu.VMEM((2, nz, STATE, D), BF16),
            pltpu.VMEM((2, nz, STATE, D), BF16),
            pltpu.VMEM((2, STATE, D), BF16),
            pltpu.VMEM((2, nx, STATE, D), BF16),
            pltpu.VMEM((2, STATE, D), BF16),
            pltpu.VMEM((2, ny, STATE, D), BF16),
            pltpu.VMEM((STATE, D), F32),
            pltpu.VMEM((2, heads, STATE, D), BF16),
            dma((4,)),
            dma((2,)),
            dma((2, nz)),
            dma((2, nz)),
            dma((2, nz)),
            dma((2, nz)),
            dma((2, nz)),
            dma((2, nx)),
            dma((2, nx)),
            dma((2, ny)),
            dma((2, ny)),
            dma((2, nz)),
            dma((2, nz)),
            dma((2, heads)),
        ],
        compiler_params=pltpu.CompilerParams(collective_id=0, has_side_effects=True),
        name="scan_attention",
    )(queries, keys, values, cotangent)


def solution(mesh):
    nz = mesh.shape["space"] // 2
    nx = int(round(mesh.shape["tm"] ** 0.5))
    ny = mesh.shape["tm"] // nx
    spec = P(("tm", "space"), None)
    return jax.shard_map(
        functools.partial(body, (nx, ny, nz)),
        mesh=mesh,
        in_specs=(spec,) * 4,
        out_specs=(spec,) * 4,
        check_vma=False,
    )
```

time: 551 us -> 84.6 us (0.15)
  waiting for transfers between devices: 279 us -> 0 us
  blocking collectives: 179 us -> 0 us
  Pallas kernels: 0 us -> 75.9 us
  other arithmetic: 31 us -> 0 us
  matrix products: 21.3 us -> 0 us
  local copies, waits for them, and re-layouts: 23.6 us -> 7.94 us
  between operations: 14.1 us -> 0.65 us
    psum x2 -> x0, waiting for transfers between devices: 250 us -> none  [combine_states(): totals = lax.psum((parts[0], parts[1], parts[2]), 'space')]
    psum x2 -> x0, blocking collectives: 94.1 us -> none  [combine_states(): totals = lax.psum((parts[0], parts[1], parts[2]), 'space')]
    all_gather x4 -> x0, blocking collectives: 84.5 us -> none  [entering(): gathered = jax.tree.map(lambda a: lax.all_gather(a, axis), part)]
    pallas_call x0 -> x1, Pallas kernels: none -> 75.9 us  [body(): pl.pallas_call(functools.partial(kernel, sizes), out_shape=(like,) * 4, i...]
    all_gather x2 -> x0, waiting for transfers between devices: 28 us -> none  [entering(): gathered = jax.tree.map(lambda a: lax.all_gather(a, axis), part)]
    add x34 -> x0, other arithmetic: 22.6 us -> none  [add_states(): return tuple((first + second for first, second in zip(earlier, later)))]
    dot_general x8 -> x0, matrix products: 21.3 us -> none  [the longest x1 4.16 us: body(): jnp.einsum('thf,hfe->the', feat_q, prefix_round, preferred_element_type=j...]
    unnamed x35 -> x10, local copies, waits for them, and re-layouts: 11.5 us -> 7.94 us
  transfers between devices with their start and end apart: 4 -> 0, of which waited for: 4 -> 0; matrix products, arithmetic and copies ran while one was open for 6% -> 0% of each run, Pallas kernels for 0% -> 0%
where the time goes in v1:
time: 84.6 us; the launch traced here: 84.5 us
  Pallas kernels  75.9 us (90%)
  local copies, waits for them, and re-layouts  7.94 us (9%)
    pallas_call x1, Pallas kernels, body(): pl.pallas_call(functools.partial(kernel, sizes), out_shape=(like,) * 4, i...  75.9 us
    unnamed x10, local copies, waits for them, and re-layouts  7.94 us

profile of v1, /device:TPU:1, one launch (start us, length us, event | category | flops | bytes accessed | tf_op | source)
XLA Modules:
  0.0 84.5 jit_solution(4522289745197490142)
XLA Ops:
  0.6 75.9 %scan_attention.1 = (bf16[384,2048]{1,0:T(8,128)(2,1)}, bf16[384,2048]{1,0:T(8,128)(2,1)}, bf16[384,2048]{1,0:T(8,128)(2,1)}, bf16[384,2048]{1,0:T(8,128)(2,1)}) custom-call(bf16[384,2048]{1,0:T(8,128)(2,1)} %q_hbm.1, bf16[384,2048]{1,0:T(8,128)(2,1)} %k_hbm.1, bf16[384,2048]{1,0:T(8,128)(2,1)} %v_hbm.1, bf16[384,2048]{1,0:T(8,128)(2,1)} %g_hbm.1), custom_call_target="tpu_custom_call" | custom-call | tf_op jit(solution)/shard_map/scan_attention/pallas_call | solution.py:378
  76.5 0.0 copy-start.2
  76.5 2.8 %copy.12 = bf16[384,2048]{1,0:T(8,128)(2,1)} copy(bf16[384,2048]{1,0:T(8,128)(2,1)} %get-tuple-element.8) | data formatting | bytes 3145728
  79.4 0.0 copy-done.2
  79.4 0.0 copy-start.1
  79.4 1.1 %copy.13 = bf16[384,2048]{1,0:T(8,128)(2,1)} copy(bf16[384,2048]{1,0:T(8,128)(2,1)S(1)} %copy-done.2) | data formatting | bytes 3145728
  80.5 0.8 copy-done.1
  81.4 0.0 copy-start
  81.4 1.1 %copy.14 = bf16[384,2048]{1,0:T(8,128)(2,1)} copy(bf16[384,2048]{1,0:T(8,128)(2,1)S(1)} %copy-done.1) | data formatting | bytes 3145728
  82.5 0.8 copy-done
  83.3 1.1 %copy.15 = bf16[384,2048]{1,0:T(8,128)(2,1)} copy(bf16[384,2048]{1,0:T(8,128)(2,1)S(1)} %copy-done) | data formatting | bytes 3145728
Async XLA Ops:
  76.5 2.9 %copy-start.2 = (bf16[384,2048]{1,0:T(8,128)(2,1)S(1)}, bf16[384,2048]{1,0:T(8,128)(2,1)}, u32[]{:S(2)}) copy-start(bf16[384,2048]{1,0:T(8,128)(2,1)} %get-tuple-element.9) | copy-start | bytes 4718596
  79.4 2.0 %copy-start.1 = (bf16[384,2048]{1,0:T(8,128)(2,1)S(1)}, bf16[384,2048]{1,0:T(8,128)(2,1)}, u32[]{:S(2)}) copy-start(bf16[384,2048]{1,0:T(8,128)(2,1)} %get-tuple-element.10) | copy-start | bytes 4718596
  81.4 2.0 %copy-start = (bf16[384,2048]{1,0:T(8,128)(2,1)S(1)}, bf16[384,2048]{1,0:T(8,128)(2,1)}, u32[]{:S(2)}) copy-start(bf16[384,2048]{1,0:T(8,128)(2,1)} %get-tuple-element.11) | copy-start | bytes 4718596

commit v2 on v1

--- a/solution.py
+++ b/solution.py
@@ -60,10 +60,10 @@
 def kernel(
     sizes,
     q_hbm, k_hbm, v_hbm, g_hbm,
-    att_hbm, gq_hbm, gk_hbm, gv_hbm,
-    q_v, k_v, v_v, g_v, att_v, gq_v, gk_v, gv_v, dnum_v, ratio_v,
-    own, pair_out, pair_in, z_out, z_in, x_out, x_in, y_out, y_in, total, fin,
-    in_sem, out_sem, grad_sem,
+    att_v, gq_v, k_v, v_v, fin1,
+    q_v, g_v, dnum_v, ratio_v,
+    own, pair_out, pair_in, z_out, z_in, x_out, x_in, y_out, y_in, total, fin0,
+    in_sem,
     pair_ss, pair_rs, z_ss, z_rs, x_ss, x_rs, y_ss, y_rs, ag_ss, fw_ss, fin_rs,
 ):
     nx, ny, nz = sizes
@@ -72,6 +72,7 @@
     z, core = lax.div(space, 2), lax.rem(space, 2)
     partner = 2 * z + 1 - core
     rows = q_v.shape[0]
+    fins = (fin0, fin1)
 
     def at_z(j):
         return 2 * j + core
@@ -130,12 +131,12 @@
 
     def gather_copy(d, j, head):
         return remote(
-            fin.at[d, head], fin.at[d, head], ag_ss.at[d, j], fin_rs.at[d, head], {"space": at_z(j)}
+            fins[d].at[head], fins[d].at[head], ag_ss.at[d, j], fin_rs.at[d, head], {"space": at_z(j)}
         )
 
     def forward_copy(d, j, head):
         return remote(
-            fin.at[d, head], fin.at[d, head], fw_ss.at[d, j], fin_rs.at[d, head], {"space": partner}
+            fins[d].at[head], fins[d].at[head], fw_ss.at[d, j], fin_rs.at[d, head], {"space": partner}
         )
 
     def give_pair(d, j, state):
@@ -162,17 +163,20 @@
         def _():
             put_packed(z_in.at[d, z], chip)
 
-    def scan(d):
+    def sum_z(d):
         group = get_state(z_in.at[d, z])
         for o in range(1, nz):
             j = lax.rem(z + o, nz)
             z_copy(d, j, j).wait_recv()
             group = group + get_state(z_in.at[d, j])
+        total[...] = group
+
+    def scan_x(d):
+        group = total[...]
         put_packed(x_out.at[d], group)
         for o in (2, 1, 3) if nx == 4 else range(1, nx):
             x_copy(d, lax.rem(x + o, nx), x).start()
         row_sum = group
-        total[...] = group
         for o in range(1, nx):
             other = lax.rem(x + o, nx)
             x_copy(d, other, other).wait_recv()
@@ -185,6 +189,8 @@
                 total[...] += block
 
         put_packed(y_out.at[d], row_sum)
+
+    def scan_y(d):
         for o in (2, 1, 3) if ny == 4 else range(1, ny):
             other = lax.rem(y + o, ny)
 
@@ -200,7 +206,8 @@
                 y_copy(d, other, other).wait_recv()
                 total[...] += get_state(y_in.at[d, other])
 
-        put_packed(fin.at[d, space], total[...])
+    def spread(d):
+        put_packed(fins[d].at[space], total[...])
         forward_copy(d, z, space).start()
 
         def send(i, carry):
@@ -249,7 +256,10 @@
     to_owner(0, order(jnp.int32(nz - 1)))
     load(2, q_hbm, q_v).wait()
     load(3, g_hbm, g_v).wait()
-    scan(0)
+    sum_z(0)
+    scan_x(0)
+    scan_y(0)
+    spread(0)
 
     count = ((tm + 1) * (rows * 2 * nz)).astype(F32)
 
@@ -258,8 +268,8 @@
         queries, grad = q_v[:, here], g_v[:, here].astype(F32)
         feat = jnp.maximum(queries, jnp.zeros_like(queries))
         feat32 = feat.astype(F32)
-        key_row, value_row = split_sums(fin[0, head, D:STATE, :].astype(F32))
-        numer = times(feat, fin[0, head, 0:D, :]) + value_row
+        key_row, value_row = split_sums(fin0[head, D:STATE, :].astype(F32))
+        numer = times(feat, fin0[head, 0:D, :]) + value_row
         denom = jnp.sum(feat32 * key_row, axis=1, keepdims=True) + count
         inverse = 1.0 / denom
         att_v[:, here] = (numer * inverse).astype(BF16)
@@ -291,46 +301,27 @@
 
     lax.fori_loop(0, nz, attend_step, 0)
     to_owner(1, order(jnp.int32(0)))
-    pltpu.make_async_copy(att_v, att_hbm, out_sem.at[0]).start()
 
     def query_step(head, carry):
         here = cols(head)
-        key_row, _ = split_sums(fin[0, head, D:STATE, :].astype(F32))
-        d_feat = times_t(dnum_v[:, here], fin[0, head, 0:D, :]) - ratio_v[head] * key_row
+        key_row, _ = split_sums(fin0[head, D:STATE, :].astype(F32))
+        d_feat = times_t(dnum_v[:, here], fin0[head, 0:D, :]) - ratio_v[head] * key_row
         gq_v[:, here] = jnp.where(q_v[:, here].astype(F32) > 0, d_feat, 0.0).astype(BF16)
         return carry
 
     lax.fori_loop(0, 2 * nz, query_step, 0)
-    pltpu.make_async_copy(gq_v, gq_hbm, out_sem.at[1]).start()
-    scan(1)
-
-    def key_value(head):
-        here = cols(head)
-        keys, values = k_v[:, here], v_v[:, here]
-        feat = jnp.maximum(keys, jnp.zeros_like(keys))
-        matrix = fin[1, head, 0:D, :]
-        key_row, value_row = split_sums(fin[1, head, D:STATE, :].astype(F32))
-        gv_v[:, here] = (times(feat, matrix) + value_row).astype(BF16)
-        d_key = times_t(values, matrix) + key_row
-        gk_v[:, here] = jnp.where(keys.astype(F32) > 0, d_key, 0.0).astype(BF16)
-
-    def grad_copy(j, which):
-        here = pl.ds(pl.multiple_of(j * 2 * D, 2 * D), 2 * D)
-        src, dst = ((gk_v, gk_hbm), (gv_v, gv_hbm))[which]
-        return pltpu.make_async_copy(src.at[:, here], dst.at[:, here], grad_sem.at[which, j])
-
-    def key_value_step(n, carry):
+    sum_z(1)
+    scan_x(1)
+    scan_y(1)
+    spread(1)
+
+    def receive_step(n, carry):
         off = order(nz - 1 - n)
-        j = lax.rem(z + off, nz)
         receive(1, off)
-        key_value(at_z(j))
         receive_pair(1, off)
-        key_value(2 * j + 1 - core)
-        grad_copy(j, 0).start()
-        grad_copy(j, 1).start()
-        return carry
-
-    lax.fori_loop(0, nz, key_value_step, 0)
+        return carry
+
+    lax.fori_loop(0, nz, receive_step, 0)
 
     for d in (0, 1):
 
@@ -357,15 +348,46 @@
             def _():
                 y_copy(d, other, y).wait_send()
 
-    pltpu.make_async_copy(att_v, att_hbm, out_sem.at[0]).wait()
-    pltpu.make_async_copy(gq_v, gq_hbm, out_sem.at[1]).wait()
+
+def finish_kernel(att_v, gq_v, k_v, v_v, fin1, att_hbm, gq_hbm, gk_hbm, gv_hbm, gk_v, gv_v, sem, grad_sem):
+    att_copy = pltpu.make_async_copy(att_v, att_hbm, sem.at[0])
+    gq_copy = pltpu.make_async_copy(gq_v, gq_hbm, sem.at[1])
+    att_copy.start()
+    gq_copy.start()
+    pairs = fin1.shape[0] // 2
+
+    def key_value(head):
+        here = cols(head)
+        keys, values = k_v[:, here], v_v[:, here]
+        feat = jnp.maximum(keys, jnp.zeros_like(keys))
+        matrix = fin1[head, 0:D, :]
+        key_row, value_row = split_sums(fin1[head, D:STATE, :].astype(F32))
+        gv_v[:, here] = (times(feat, matrix) + value_row).astype(BF16)
+        d_key = times_t(values, matrix) + key_row
+        gk_v[:, here] = jnp.where(keys.astype(F32) > 0, d_key, 0.0).astype(BF16)
+
+    def grad_copy(j, which):
+        here = pl.ds(pl.multiple_of(j * 2 * D, 2 * D), 2 * D)
+        src, dst = ((gk_v, gk_hbm), (gv_v, gv_hbm))[which]
+        return pltpu.make_async_copy(src.at[:, here], dst.at[:, here], grad_sem.at[which, j])
+
+    def step(j, carry):
+        key_value(2 * j)
+        key_value(2 * j + 1)
+        grad_copy(j, 0).start()
+        grad_copy(j, 1).start()
+        return carry
+
+    lax.fori_loop(0, pairs, step, 0)
+    att_copy.wait()
+    gq_copy.wait()
 
     def stored(j, carry):
         grad_copy(j, 0).wait()
         grad_copy(j, 1).wait()
         return carry
 
-    lax.fori_loop(0, nz, stored, 0)
+    lax.fori_loop(0, pairs, stored, 0)
 
 
 def body(sizes, queries, keys, values, cotangent):
@@ -375,12 +397,14 @@
     whole = pltpu.VMEM((rows, width), BF16)
     dma = pltpu.SemaphoreType.DMA
     like = jax.ShapeDtypeStruct((rows, width), BF16)
-    return pl.pallas_call(
+    in_vmem = pl.BlockSpec(memory_space=pltpu.VMEM)
+    in_hbm = pl.BlockSpec(memory_space=pl.ANY)
+    held = pl.pallas_call(
         functools.partial(kernel, sizes),
-        out_shape=(like,) * 4,
-        in_specs=[pl.BlockSpec(memory_space=pl.ANY)] * 4,
-        out_specs=(pl.BlockSpec(memory_space=pl.ANY),) * 4,
-        scratch_shapes=[whole] * 9
+        out_shape=(whole,) * 4 + (pltpu.VMEM((heads, STATE, D), BF16),),
+        in_specs=[pl.BlockSpec(memory_space=pltpu.HBM)] * 4,
+        out_specs=(in_vmem,) * 5,
+        scratch_shapes=[whole] * 3
         + [
             pltpu.VMEM((heads, rows, 1), F32),
             pltpu.VMEM((nz, STATE, D), F32),
@@ -393,10 +417,8 @@
             pltpu.VMEM((2, STATE, D), BF16),
             pltpu.VMEM((2, ny, STATE, D), BF16),
             pltpu.VMEM((STATE, D), F32),
-            pltpu.VMEM((2, heads, STATE, D), BF16),
+            pltpu.VMEM((heads, STATE, D), BF16),
             dma((4,)),
-            dma((2,)),
-            dma((2, nz)),
             dma((2, nz)),
             dma((2, nz)),
             dma((2, nz)),
@@ -409,9 +431,20 @@
             dma((2, nz)),
             dma((2, heads)),
         ],
-        compiler_params=pltpu.CompilerParams(collective_id=0, has_side_effects=True),
+        compiler_params=pltpu.CompilerParams(
+            collective_id=0, has_side_effects=True, vmem_limit_bytes=32 << 20
+        ),
         name="scan_attention",
-    )(queries, keys, values, cotangent)
+    )(*(pltpu.with_memory_space_constraint(a, pltpu.HBM) for a in (queries, keys, values, cotangent)))
+    return pl.pallas_call(
+        finish_kernel,
+        out_shape=(like,) * 4,
+        in_specs=[in_vmem] * 5,
+        out_specs=(in_hbm,) * 4,
+        scratch_shapes=[whole] * 2 + [dma((2,)), dma((2, nz))],
+        compiler_params=pltpu.CompilerParams(vmem_limit_bytes=16 << 20),
+        name="finish",
+    )(*held)
 
 
 def solution(mesh):

time: 84.6 us -> 77.6 us (0.917)
  local copies, waits for them, and re-layouts: 7.94 us -> 0 us
  Pallas kernels: 75.9 us -> 76.9 us
    unnamed x10 -> x0, local copies, waits for them, and re-layouts: 7.94 us -> none
    pallas_call x1 -> x2, Pallas kernels: 75.9 us -> 76.9 us  [the longest x1 73.6 us: body(): pl.pallas_call(functools.partial(kernel, sizes), out_shape=(whole,) * 4 +...]
where the time goes in v2:
time: 77.6 us; the launch traced here: 77.5 us
  Pallas kernels  76.9 us (99%)
    pallas_call x1, Pallas kernels, body(): pl.pallas_call(functools.partial(kernel, sizes), out_shape=(whole,) * 4 +...  73.6 us
    pallas_call x1, Pallas kernels, body(): pl.pallas_call(finish_kernel, out_shape=(like,) * 4, in_specs=[in_vmem] *...  3.27 us

profile of v2, /device:TPU:1, one launch (start us, length us, event | category | flops | bytes accessed | tf_op | source)
XLA Modules:
  0.0 77.5 jit_solution(12030812577397211575)
XLA Ops:
  0.6 73.6 %scan_attention.1 = (bf16[384,2048]{1,0:T(8,128)(2,1)S(1)}, bf16[384,2048]{1,0:T(8,128)(2,1)S(1)}, bf16[384,2048]{1,0:T(8,128)(2,1)S(1)}, bf16[384,2048]{1,0:T(8,128)(2,1)S(1)}, bf16[16,144,128]{2,1,0:T(8,128)(2,1)S(1)}) custom-call(bf16[384,2048]{1,0:T(8,128)(2,1)} %q_hbm.1, bf16[384,2048]{1,0:T(8,128)(2,1)} %k_hbm.1, bf16[384,2048]{1,0:T(8,128)(2,1)} %v_hbm.1, ...), custom_call_target="tpu_custom_call" | custom-call | tf_op jit(solution)/shard_map/scan_attention/pallas_call | solution.py:402
  74.3 3.3 %finish.1 = (bf16[384,2048]{1,0:T(8,128)(2,1)}, bf16[384,2048]{1,0:T(8,128)(2,1)}, bf16[384,2048]{1,0:T(8,128)(2,1)}, bf16[384,2048]{1,0:T(8,128)(2,1)}) custom-call(bf16[384,2048]{1,0:T(8,128)(2,1)S(1)} %get-tuple-element.9.att_v, bf16[384,2048]{1,0:T(8,128)(2,1)S(1)} %get-tuple-element.10.gq_v, bf16[384,2048]{1,0:T(8,128)(2,1)S(1)} %get-tuple-element.11.k_v, ...), custom_call_target="tpu_custom_call" | custom-call | tf_op jit(solution)/shard_map/finish/pallas_call | solution.py:439

commit v3 on v2

--- a/solution.py
+++ b/solution.py
@@ -60,9 +60,9 @@
 def kernel(
     sizes,
     q_hbm, k_hbm, v_hbm, g_hbm,
-    att_v, gq_v, k_v, v_v, fin1,
-    q_v, g_v, dnum_v, ratio_v,
-    own, pair_out, pair_in, z_out, z_in, x_out, x_in, y_out, y_in, total, fin0,
+    att_v, gq_v, gk_v, gv_v,
+    q_v, k_v, v_v, g_v, dnum_v, ratio_v,
+    own, pair_out, pair_in, z_out, z_in, x_out, x_in, y_out, y_in, total, fin0, fin1,
     in_sem,
     pair_ss, pair_rs, z_ss, z_rs, x_ss, x_rs, y_ss, y_rs, ag_ss, fw_ss, fin_rs,
 ):
@@ -230,7 +230,6 @@
 
     load(0, k_hbm, k_v).wait()
     load(1, v_hbm, v_v).wait()
-    pl.semaphore_wait(barrier, 1 + (nz - 1) + (nx - 1) + (ny - 1))
 
     def state_of(head):
         keys, values = k_v[:, cols(head)], v_v[:, cols(head)]
@@ -241,19 +240,27 @@
             jnp.sum(values.astype(F32), axis=0, keepdims=True),
         )
 
-    def state_step(i, carry):
-        j = lax.rem(z + order(i), nz)
-        give_pair(0, j, state_of(2 * j + 1 - core))
+    def pair_step(j, carry):
+        put_state(pair_out.at[0, j], *state_of(2 * j + 1 - core))
+        return carry
+
+    lax.fori_loop(0, nz, pair_step, 0)
+    pl.semaphore_wait(barrier, 1 + (nz - 1) + (nx - 1) + (ny - 1))
+
+    def pair_send(i, carry):
+        pair_copy(0, lax.rem(z + order(i), nz)).start()
+        return carry
+
+    lax.fori_loop(0, nz, pair_send, 0)
+
+    def own_step(i, carry):
+        off = order(i)
+        j = lax.rem(z + off, nz)
         keep_own(j, state_of(at_z(j)))
-
-        @pl.when(i > 0)
-        def _():
-            to_owner(0, order(i - 1))
-
-        return carry
-
-    lax.fori_loop(0, nz, state_step, 0)
-    to_owner(0, order(jnp.int32(nz - 1)))
+        to_owner(0, off)
+        return carry
+
+    lax.fori_loop(0, nz, own_step, 0)
     load(2, q_hbm, q_v).wait()
     load(3, g_hbm, g_v).wait()
     sum_z(0)
@@ -284,22 +291,33 @@
             jnp.sum(dnum, axis=0, keepdims=True),
         )
 
+    def attend_own(n):
+        off = order(nz - 1 - n)
+        receive(0, off)
+        j = lax.rem(z + off, nz)
+        keep_own(j, attend(at_z(j)))
+
+    def attend_pair(n):
+        off = order(nz - 1 - n)
+        receive_pair(0, off)
+        j = lax.rem(z + off, nz)
+        give_pair(1, j, attend(2 * j + 1 - core))
+
+    attend_own(jnp.int32(0))
+
     def attend_step(n, carry):
-        i = nz - 1 - n
-        off = order(i)
-        j = lax.rem(z + off, nz)
-        receive(0, off)
-        keep_own(j, attend(at_z(j)))
-        receive_pair(0, off)
-        give_pair(1, j, attend(2 * j + 1 - core))
-
-        @pl.when(n > 0)
+        attend_own(n)
+        attend_pair(n - 1)
+
+        @pl.when(n > 1)
         def _():
-            to_owner(1, order(i + 1))
-
-        return carry
-
-    lax.fori_loop(0, nz, attend_step, 0)
+            to_owner(1, order(nz + 1 - n))
+
+        return carry
+
+    lax.fori_loop(1, nz, attend_step, 0)
+    attend_pair(jnp.int32(nz - 1))
+    to_owner(1, order(jnp.int32(1)))
     to_owner(1, order(jnp.int32(0)))
 
     def query_step(head, carry):
@@ -314,47 +332,6 @@
     scan_x(1)
     scan_y(1)
     spread(1)
-
-    def receive_step(n, carry):
-        off = order(nz - 1 - n)
-        receive(1, off)
-        receive_pair(1, off)
-        return carry
-
-    lax.fori_loop(0, nz, receive_step, 0)
-
-    for d in (0, 1):
-
-        def sent(i, carry):
-            off = order(i)
-            j = lax.rem(z + off, nz)
-            pair_copy(d, j).wait_send()
-            forward_copy(d, j, at_z(j)).wait_send()
-
-            @pl.when(off != 0)
-            def _():
-                z_copy(d, j, z).wait_send()
-                gather_copy(d, j, space).wait_send()
-
-            return carry
-
-        lax.fori_loop(0, nz, sent, 0)
-        for o in range(1, nx):
-            x_copy(d, lax.rem(x + o, nx), x).wait_send()
-        for o in range(1, ny):
-            other = lax.rem(y + o, ny)
-
-            @pl.when(other > y if d == 0 else other < y)
-            def _():
-                y_copy(d, other, y).wait_send()
-
-
-def finish_kernel(att_v, gq_v, k_v, v_v, fin1, att_hbm, gq_hbm, gk_hbm, gv_hbm, gk_v, gv_v, sem, grad_sem):
-    att_copy = pltpu.make_async_copy(att_v, att_hbm, sem.at[0])
-    gq_copy = pltpu.make_async_copy(gq_v, gq_hbm, sem.at[1])
-    att_copy.start()
-    gq_copy.start()
-    pairs = fin1.shape[0] // 2
 
     def key_value(head):
         here = cols(head)
@@ -366,28 +343,65 @@
         d_key = times_t(values, matrix) + key_row
         gk_v[:, here] = jnp.where(keys.astype(F32) > 0, d_key, 0.0).astype(BF16)
 
-    def grad_copy(j, which):
-        here = pl.ds(pl.multiple_of(j * 2 * D, 2 * D), 2 * D)
-        src, dst = ((gk_v, gk_hbm), (gv_v, gv_hbm))[which]
-        return pltpu.make_async_copy(src.at[:, here], dst.at[:, here], grad_sem.at[which, j])
-
-    def step(j, carry):
-        key_value(2 * j)
-        key_value(2 * j + 1)
-        grad_copy(j, 0).start()
-        grad_copy(j, 1).start()
-        return carry
-
-    lax.fori_loop(0, pairs, step, 0)
-    att_copy.wait()
-    gq_copy.wait()
-
-    def stored(j, carry):
-        grad_copy(j, 0).wait()
-        grad_copy(j, 1).wait()
-        return carry
-
-    lax.fori_loop(0, pairs, stored, 0)
+    def grads_own(n):
+        off = order(nz - 1 - n)
+        receive(1, off)
+        key_value(at_z(lax.rem(z + off, nz)))
+
+    def grads_pair(n):
+        off = order(nz - 1 - n)
+        receive_pair(1, off)
+        key_value(2 * lax.rem(z + off, nz) + 1 - core)
+
+    grads_own(jnp.int32(0))
+
+    def grads_step(n, carry):
+        grads_own(n)
+        grads_pair(n - 1)
+        return carry
+
+    lax.fori_loop(1, nz, grads_step, 0)
+    grads_pair(jnp.int32(nz - 1))
+
+    for d in (0, 1):
+
+        def sent(i, carry):
+            off = order(i)
+            j = lax.rem(z + off, nz)
+            pair_copy(d, j).wait_send()
+            forward_copy(d, j, at_z(j)).wait_send()
+
+            @pl.when(off != 0)
+            def _():
+                z_copy(d, j, z).wait_send()
+                gather_copy(d, j, space).wait_send()
+
+            return carry
+
+        lax.fori_loop(0, nz, sent, 0)
+        for o in range(1, nx):
+            x_copy(d, lax.rem(x + o, nx), x).wait_send()
+        for o in range(1, ny):
+            other = lax.rem(y + o, ny)
+
+            @pl.when(other > y if d == 0 else other < y)
+            def _():
+                y_copy(d, other, y).wait_send()
+
+
+def store_kernel(*refs):
+    count = (len(refs) - 1) // 2
+    sources, targets, sem = refs[:count], refs[count : 2 * count], refs[-1]
+    half = sources[0].shape[0] // 2
+    copies = [
+        pltpu.make_async_copy(src.at[pl.ds(part * half, half)], dst.at[pl.ds(part * half, half)], sem.at[n, part])
+        for n, (src, dst) in enumerate(zip(sources, targets))
+        for part in range(2)
+    ]
+    for copy in copies:
+        copy.start()
+    for copy in copies:
+        copy.wait()
 
 
 def body(sizes, queries, keys, values, cotangent):
@@ -401,10 +415,10 @@
     in_hbm = pl.BlockSpec(memory_space=pl.ANY)
     held = pl.pallas_call(
         functools.partial(kernel, sizes),
-        out_shape=(whole,) * 4 + (pltpu.VMEM((heads, STATE, D), BF16),),
+        out_shape=(whole,) * 4,
         in_specs=[pl.BlockSpec(memory_space=pltpu.HBM)] * 4,
-        out_specs=(in_vmem,) * 5,
-        scratch_shapes=[whole] * 3
+        out_specs=(in_vmem,) * 4,
+        scratch_shapes=[whole] * 5
         + [
             pltpu.VMEM((heads, rows, 1), F32),
             pltpu.VMEM((nz, STATE, D), F32),
@@ -418,6 +432,7 @@
             pltpu.VMEM((2, ny, STATE, D), BF16),
             pltpu.VMEM((STATE, D), F32),
             pltpu.VMEM((heads, STATE, D), BF16),
+            pltpu.VMEM((heads, STATE, D), BF16),
             dma((4,)),
             dma((2, nz)),
             dma((2, nz)),
@@ -437,13 +452,13 @@
         name="scan_attention",
     )(*(pltpu.with_memory_space_constraint(a, pltpu.HBM) for a in (queries, keys, values, cotangent)))
     return pl.pallas_call(
-        finish_kernel,
+        store_kernel,
         out_shape=(like,) * 4,
-        in_specs=[in_vmem] * 5,
+        in_specs=[in_vmem] * 4,
         out_specs=(in_hbm,) * 4,
-        scratch_shapes=[whole] * 2 + [dma((2,)), dma((2, nz))],
+        scratch_shapes=[dma((4, 2))],
         compiler_params=pltpu.CompilerParams(vmem_limit_bytes=16 << 20),
-        name="finish",
+        name="store",
     )(*held)
 
 

time: 77.6 us -> 73.8 us (0.951)
  Pallas kernels: 76.9 us -> 73.1 us
    pallas_call x2, Pallas kernels: 76.9 us -> 73.1 us  [the longest x1 70.3 us: body(): pl.pallas_call(functools.partial(kernel, sizes), out_shape=(whole,) * 4,...]
where the time goes in v3:
time: 73.8 us; the launch traced here: 73.7 us
  Pallas kernels  73.1 us (99%)
    pallas_call x1, Pallas kernels, body(): pl.pallas_call(functools.partial(kernel, sizes), out_shape=(whole,) * 4,...  70.3 us
    pallas_call x1, Pallas kernels, body(): pl.pallas_call(store_kernel, out_shape=(like,) * 4, in_specs=[in_vmem] *...  2.74 us

profile of v3, /device:TPU:1, one launch (start us, length us, event | category | flops | bytes accessed | tf_op | source)
XLA Modules:
  0.0 73.7 jit_solution(17377922098317035763)
XLA Ops:
  0.6 70.3 %scan_attention.1 = (bf16[384,2048]{1,0:T(8,128)(2,1)S(1)}, bf16[384,2048]{1,0:T(8,128)(2,1)S(1)}, bf16[384,2048]{1,0:T(8,128)(2,1)S(1)}, bf16[384,2048]{1,0:T(8,128)(2,1)S(1)}) custom-call(bf16[384,2048]{1,0:T(8,128)(2,1)} %q_hbm.1, bf16[384,2048]{1,0:T(8,128)(2,1)} %k_hbm.1, bf16[384,2048]{1,0:T(8,128)(2,1)} %v_hbm.1, bf16[384,2048]{1,0:T(8,128)(2,1)} %g_hbm.1), custom_call_target="tpu_custom_call" | custom-call | tf_op jit(solution)/shard_map/scan_attention/pallas_call | solution.py:416
  71.0 2.7 %store.1 = (bf16[384,2048]{1,0:T(8,128)(2,1)}, bf16[384,2048]{1,0:T(8,128)(2,1)}, bf16[384,2048]{1,0:T(8,128)(2,1)}, bf16[384,2048]{1,0:T(8,128)(2,1)}) custom-call(bf16[384,2048]{1,0:T(8,128)(2,1)S(1)} %get-tuple-element.8.refs_0_, bf16[384,2048]{1,0:T(8,128)(2,1)S(1)} %get-tuple-element.9.refs_1_, bf16[384,2048]{1,0:T(8,128)(2,1)S(1)} %get-tuple-element.10.refs_2_, ...), custom_call_target="tpu_custom_call" | custom-call | tf_op jit(solution)/shard_map/store/pallas_call | solution.py:454

commit v4 on v3

--- a/solution.py
+++ b/solution.py
@@ -9,6 +9,8 @@
 
 D = 128
 STATE = D + 16
+PARTS = ((0, 64), (64, STATE - 64))
+LAG = 3
 MESH = pl.DeviceIdType.MESH
 F32 = jnp.float32
 BF16 = jnp.bfloat16
@@ -36,13 +38,22 @@
     ref[D:STATE, :] = sums_tile(key_row, value_row)
 
 
-def get_state(ref):
-    return ref[...].astype(F32)
-
-
 def put_packed(ref, packed):
-    key_row, value_row = split_sums(packed[D:STATE])
-    put_state(ref, packed[0:D], key_row, value_row)
+    for part, (start, size) in enumerate(PARTS):
+        put_part(ref, part, packed[start : start + size])
+
+
+def put_part(ref, part, packed):
+    start, size = PARTS[part]
+    stop = min(start + size, D)
+    ref[start:stop, :] = packed[: stop - start].astype(BF16)
+    if start + size > D:
+        ref[D:STATE, :] = sums_tile(*split_sums(packed[stop - start :]))
+
+
+def get_part(ref, part):
+    start, size = PARTS[part]
+    return ref[start : start + size, :].astype(F32)
 
 
 def across(left, right):
@@ -64,7 +75,7 @@
     q_v, k_v, v_v, g_v, dnum_v, ratio_v,
     own, pair_out, pair_in, z_out, z_in, x_out, x_in, y_out, y_in, total, fin0, fin1,
     in_sem,
-    pair_ss, pair_rs, z_ss, z_rs, x_ss, x_rs, y_ss, y_rs, ag_ss, fw_ss, fin_rs,
+    pair_ss, pair_rs, z_ss, z_rs, x_ss, x_rs, y_ss, y_rs, ag_ss, ag_rs, fw_ss, fw_rs,
 ):
     nx, ny, nz = sizes
     tm, space = lax.axis_index("tm"), lax.axis_index("space")
@@ -114,30 +125,34 @@
             pair_out.at[d, j], pair_in.at[d, j], pair_ss.at[d, j], pair_rs.at[d, j], {"space": partner}
         )
 
-    def z_copy(d, j, slot):
+    def z_copy(d, part, j, slot):
+        rows_of = pl.ds(*PARTS[part])
         return remote(
-            z_out.at[d, j], z_in.at[d, slot], z_ss.at[d, j], z_rs.at[d, slot], {"space": at_z(j)}
-        )
-
-    def x_copy(d, other, slot):
+            z_out.at[d, j, rows_of], z_in.at[d, slot, rows_of],
+            z_ss.at[d, part, j], z_rs.at[d, part, slot], {"space": at_z(j)},
+        )
+
+    def x_copy(d, part, other, slot):
+        rows_of = pl.ds(*PARTS[part])
         return remote(
-            x_out.at[d], x_in.at[d, slot], x_ss.at[d, other], x_rs.at[d, slot], {"tm": y * nx + other}
-        )
-
-    def y_copy(d, other, slot):
+            x_out.at[d, rows_of], x_in.at[d, slot, rows_of],
+            x_ss.at[d, part, other], x_rs.at[d, part, slot], {"tm": y * nx + other},
+        )
+
+    def y_copy(d, part, other, slot):
+        rows_of = pl.ds(*PARTS[part])
         return remote(
-            y_out.at[d], y_in.at[d, slot], y_ss.at[d, other], y_rs.at[d, slot], {"tm": other * nx + x}
-        )
-
-    def gather_copy(d, j, head):
-        return remote(
-            fins[d].at[head], fins[d].at[head], ag_ss.at[d, j], fin_rs.at[d, head], {"space": at_z(j)}
-        )
+            y_out.at[d, rows_of], y_in.at[d, slot, rows_of],
+            y_ss.at[d, part, other], y_rs.at[d, part, slot], {"tm": other * nx + x},
+        )
+
+    def gather_copy(d, part, j, head):
+        here = fins[d].at[head, pl.ds(*PARTS[part])]
+        return remote(here, here, ag_ss.at[d, part, j], ag_rs.at[d, part, head], {"space": at_z(j)})
 
     def forward_copy(d, j, head):
-        return remote(
-            fins[d].at[head], fins[d].at[head], fw_ss.at[d, j], fin_rs.at[d, head], {"space": partner}
-        )
+        here = fins[d].at[head]
+        return remote(here, here, fw_ss.at[d, j], fw_rs.at[d, head], {"space": partner})
 
     def give_pair(d, j, state):
         put_state(pair_out.at[d, j], *state)
@@ -149,84 +164,93 @@
         own[j, 0:D, :] = matrix
         own[j, D:STATE, :] = jnp.where(row == 0, key_row, jnp.where(row == 2, value_row, 0.0))
 
-    def to_owner(d, off):
+    def to_owner(d, off, parts):
         j = lax.rem(z + off, nz)
         pair_copy(d, j).wait_recv()
-        chip = own[j] + get_state(pair_in.at[d, j])
+        chip = own[j] + pair_in[d, j].astype(F32)
 
         @pl.when(off != 0)
         def _():
             put_packed(z_out.at[d, j], chip)
-            z_copy(d, j, z).start()
+            for part in range(parts):
+                z_copy(d, part, j, z).start()
 
         @pl.when(off == 0)
         def _():
             put_packed(z_in.at[d, z], chip)
 
-    def sum_z(d):
-        group = get_state(z_in.at[d, z])
+    def sum_z(d, part):
+        start, size = PARTS[part]
+        group = get_part(z_in.at[d, z], part)
         for o in range(1, nz):
             j = lax.rem(z + o, nz)
-            z_copy(d, j, j).wait_recv()
-            group = group + get_state(z_in.at[d, j])
-        total[...] = group
-
-    def scan_x(d):
-        group = total[...]
-        put_packed(x_out.at[d], group)
+            z_copy(d, part, j, j).wait_recv()
+            group = group + get_part(z_in.at[d, j], part)
+        put_part(x_out.at[d], part, group)
         for o in (2, 1, 3) if nx == 4 else range(1, nx):
-            x_copy(d, lax.rem(x + o, nx), x).start()
-        row_sum = group
+            x_copy(d, part, lax.rem(x + o, nx), x).start()
+        total[start : start + size, :] = group
+
+    def scan_x(d, part):
+        start, size = PARTS[part]
+        row_sum = total[start : start + size, :]
         for o in range(1, nx):
             other = lax.rem(x + o, nx)
-            x_copy(d, other, other).wait_recv()
-            block = get_state(x_in.at[d, other])
+            x_copy(d, part, other, other).wait_recv()
+            block = get_part(x_in.at[d, other], part)
             row_sum = row_sum + block
-            before = other < x if d == 0 else other > x
-
-            @pl.when(before)
+
+            @pl.when(other < x if d == 0 else other > x)
             def _():
-                total[...] += block
-
-        put_packed(y_out.at[d], row_sum)
-
-    def scan_y(d):
+                total[start : start + size, :] += block
+
+        put_part(y_out.at[d], part, row_sum)
         for o in (2, 1, 3) if ny == 4 else range(1, ny):
             other = lax.rem(y + o, ny)
 
             @pl.when(other > y if d == 0 else other < y)
             def _():
-                y_copy(d, other, y).start()
-
+                y_copy(d, part, other, y).start()
+
+    def scan_y(d, part):
+        start, size = PARTS[part]
         for o in range(1, ny):
             other = lax.rem(y + o, ny)
 
             @pl.when(other < y if d == 0 else other > y)
             def _():
-                y_copy(d, other, other).wait_recv()
-                total[...] += get_state(y_in.at[d, other])
-
-    def spread(d):
-        put_packed(fins[d].at[space], total[...])
+                y_copy(d, part, other, other).wait_recv()
+                total[start : start + size, :] += get_part(y_in.at[d, other], part)
+
+        put_part(fins[d].at[space], part, total[start : start + size, :])
+
+        def send(i, carry):
+            gather_copy(d, part, lax.rem(z + order(i), nz), space).start()
+            return carry
+
+        lax.fori_loop(0, nz - 1, send, 0)
+
+    def scan(d):
+        for stage in (sum_z, scan_x, scan_y):
+            for part in range(len(PARTS)):
+                stage(d, part)
         forward_copy(d, z, space).start()
-
-        def send(i, carry):
-            gather_copy(d, lax.rem(z + order(i), nz), space).start()
-            return carry
-
-        lax.fori_loop(0, nz - 1, send, 0)
 
     def receive(d, off):
         j = lax.rem(z + off, nz)
 
         @pl.when(off != 0)
         def _():
-            gather_copy(d, j, at_z(j)).wait_recv()
+            for part in range(len(PARTS)):
+                gather_copy(d, part, j, at_z(j)).wait_recv()
             forward_copy(d, j, at_z(j)).start()
 
     def receive_pair(d, off):
         j = lax.rem(z + off, nz)
         forward_copy(d, j, 2 * j + 1 - core).wait_recv()
+
+    def arrival(n):
+        return jnp.where(n == 0, 0, order(n - 1))
 
     load(0, k_hbm, k_v).wait()
     load(1, v_hbm, v_v).wait()
@@ -257,16 +281,20 @@
         off = order(i)
         j = lax.rem(z + off, nz)
         keep_own(j, state_of(at_z(j)))
-        to_owner(0, off)
+        to_owner(0, off, 1)
         return carry
 
     lax.fori_loop(0, nz, own_step, 0)
+
+    def rest_send(i, carry):
+        for part in range(1, len(PARTS)):
+            z_copy(0, part, lax.rem(z + order(i), nz), z).start()
+        return carry
+
+    lax.fori_loop(0, nz - 1, rest_send, 0)
     load(2, q_hbm, q_v).wait()
     load(3, g_hbm, g_v).wait()
-    sum_z(0)
-    scan_x(0)
-    scan_y(0)
-    spread(0)
+    scan(0)
 
     count = ((tm + 1) * (rows * 2 * nz)).astype(F32)
 
@@ -291,34 +319,28 @@
             jnp.sum(dnum, axis=0, keepdims=True),
         )
 
-    def attend_own(n):
-        off = order(nz - 1 - n)
-        receive(0, off)
-        j = lax.rem(z + off, nz)
-        keep_own(j, attend(at_z(j)))
-
-    def attend_pair(n):
-        off = order(nz - 1 - n)
-        receive_pair(0, off)
-        j = lax.rem(z + off, nz)
-        give_pair(1, j, attend(2 * j + 1 - core))
-
-    attend_own(jnp.int32(0))
-
     def attend_step(n, carry):
-        attend_own(n)
-        attend_pair(n - 1)
-
-        @pl.when(n > 1)
-        def _():
-            to_owner(1, order(nz + 1 - n))
-
-        return carry
-
-    lax.fori_loop(1, nz, attend_step, 0)
-    attend_pair(jnp.int32(nz - 1))
-    to_owner(1, order(jnp.int32(1)))
-    to_owner(1, order(jnp.int32(0)))
+        @pl.when(n < nz)
+        def _():
+            off = arrival(n)
+            receive(0, off)
+            j = lax.rem(z + off, nz)
+            keep_own(j, attend(at_z(j)))
+
+        @pl.when((n >= LAG) & (n < nz + LAG))
+        def _():
+            off = arrival(n - LAG)
+            receive_pair(0, off)
+            j = lax.rem(z + off, nz)
+            give_pair(1, j, attend(2 * j + 1 - core))
+
+        @pl.when(n >= 2 * LAG)
+        def _():
+            to_owner(1, arrival(n - 2 * LAG), len(PARTS))
+
+        return carry
+
+    lax.fori_loop(0, nz + 2 * LAG, attend_step, 0)
 
     def query_step(head, carry):
         here = cols(head)
@@ -328,10 +350,7 @@
         return carry
 
     lax.fori_loop(0, 2 * nz, query_step, 0)
-    sum_z(1)
-    scan_x(1)
-    scan_y(1)
-    spread(1)
+    scan(1)
 
     def key_value(head):
         here = cols(head)
@@ -343,25 +362,22 @@
         d_key = times_t(values, matrix) + key_row
         gk_v[:, here] = jnp.where(keys.astype(F32) > 0, d_key, 0.0).astype(BF16)
 
-    def grads_own(n):
-        off = order(nz - 1 - n)
-        receive(1, off)
-        key_value(at_z(lax.rem(z + off, nz)))
-
-    def grads_pair(n):
-        off = order(nz - 1 - n)
-        receive_pair(1, off)
-        key_value(2 * lax.rem(z + off, nz) + 1 - core)
-
-    grads_own(jnp.int32(0))
-
     def grads_step(n, carry):
-        grads_own(n)
-        grads_pair(n - 1)
-        return carry
-
-    lax.fori_loop(1, nz, grads_step, 0)
-    grads_pair(jnp.int32(nz - 1))
+        @pl.when(n < nz)
+        def _():
+            off = arrival(n)
+            receive(1, off)
+            key_value(at_z(lax.rem(z + off, nz)))
+
+        @pl.when(n >= LAG)
+        def _():
+            off = arrival(n - LAG)
+            receive_pair(1, off)
+            key_value(2 * lax.rem(z + off, nz) + 1 - core)
+
+        return carry
+
+    lax.fori_loop(0, nz + LAG, grads_step, 0)
 
     for d in (0, 1):
 
@@ -373,20 +389,23 @@
 
             @pl.when(off != 0)
             def _():
-                z_copy(d, j, z).wait_send()
-                gather_copy(d, j, space).wait_send()
+                for part in range(len(PARTS)):
+                    z_copy(d, part, j, z).wait_send()
+                    gather_copy(d, part, j, space).wait_send()
 
             return carry
 
         lax.fori_loop(0, nz, sent, 0)
         for o in range(1, nx):
-            x_copy(d, lax.rem(x + o, nx), x).wait_send()
+            for part in range(len(PARTS)):
+                x_copy(d, part, lax.rem(x + o, nx), x).wait_send()
         for o in range(1, ny):
             other = lax.rem(y + o, ny)
 
             @pl.when(other > y if d == 0 else other < y)
             def _():
-                y_copy(d, other, y).wait_send()
+                for part in range(len(PARTS)):
+                    y_copy(d, part, other, y).wait_send()
 
 
 def store_kernel(*refs):
@@ -436,13 +455,14 @@
             dma((4,)),
             dma((2, nz)),
             dma((2, nz)),
-            dma((2, nz)),
-            dma((2, nz)),
-            dma((2, nx)),
-            dma((2, nx)),
-            dma((2, ny)),
-            dma((2, ny)),
-            dma((2, nz)),
+            dma((2, 2, nz)),
+            dma((2, 2, nz)),
+            dma((2, 2, nx)),
+            dma((2, 2, nx)),
+            dma((2, 2, ny)),
+            dma((2, 2, ny)),
+            dma((2, 2, nz)),
+            dma((2, 2, heads)),
             dma((2, nz)),
             dma((2, heads)),
         ],

time: 73.8 us -> 69.1 us (0.936)
  Pallas kernels: 73.1 us -> 68.4 us
    pallas_call x1, Pallas kernels: 70.3 us -> 65.6 us  [body(): pl.pallas_call(functools.partial(kernel, sizes), out_shape=(whole,) * 4,...]
where the time goes in v4:
time: 69.1 us; the launch traced here: 69 us
  Pallas kernels  68.4 us (99%)
    pallas_call x1, Pallas kernels, body(): pl.pallas_call(functools.partial(kernel, sizes), out_shape=(whole,) * 4,...  65.6 us
    pallas_call x1, Pallas kernels, body(): pl.pallas_call(store_kernel, out_shape=(like,) * 4, in_specs=[in_vmem] *...  2.74 us

profile of v4, /device:TPU:1, one launch (start us, length us, event | category | flops | bytes accessed | tf_op | source)
XLA Modules:
  0.0 69.0 jit_solution(15810912083727805214)
XLA Ops:
  0.6 65.6 %scan_attention.1 = (bf16[384,2048]{1,0:T(8,128)(2,1)S(1)}, bf16[384,2048]{1,0:T(8,128)(2,1)S(1)}, bf16[384,2048]{1,0:T(8,128)(2,1)S(1)}, bf16[384,2048]{1,0:T(8,128)(2,1)S(1)}) custom-call(bf16[384,2048]{1,0:T(8,128)(2,1)} %q_hbm.1, bf16[384,2048]{1,0:T(8,128)(2,1)} %k_hbm.1, bf16[384,2048]{1,0:T(8,128)(2,1)} %v_hbm.1, bf16[384,2048]{1,0:T(8,128)(2,1)} %g_hbm.1), custom_call_target="tpu_custom_call" | custom-call | tf_op jit(solution)/shard_map/scan_attention/pallas_call | solution.py:435
  66.3 2.7 %store.1 = (bf16[384,2048]{1,0:T(8,128)(2,1)}, bf16[384,2048]{1,0:T(8,128)(2,1)}, bf16[384,2048]{1,0:T(8,128)(2,1)}, bf16[384,2048]{1,0:T(8,128)(2,1)}) custom-call(bf16[384,2048]{1,0:T(8,128)(2,1)S(1)} %get-tuple-element.8.refs_0_, bf16[384,2048]{1,0:T(8,128)(2,1)S(1)} %get-tuple-element.9.refs_1_, bf16[384,2048]{1,0:T(8,128)(2,1)S(1)} %get-tuple-element.10.refs_2_, ...), custom_call_target="tpu_custom_call" | custom-call | tf_op jit(solution)/shard_map/store/pallas_call | solution.py:474
